TPU v7x, 32 devices: a whole 2x2x4 slice. The times are simulated.
32 devices in a mesh: kz: 8 (over z, x), en: 4 (over y, core).
Axes of the slice: x: 2, y: 2, z: 4, core: 2. Of those that a mesh axis runs over, the one named last changes fastest.
Arguments:
- green_real: bfloat16 [8, 96, 128, 128], P('kz', 'en'), may hold values from -6 to 6
- green_imag: bfloat16 [8, 96, 128, 128], P('kz', 'en'), may hold values from -6 to 6
- coupling: bfloat16 [2, 4, 8, 128, 128], P(None, None, 'kz'), may hold values from -0.5 to 0.5
- strengths: float32 [2, 4, 8], replicated, may hold values from 0.1 to 1
- offsets: int32 [2, 8], replicated, may hold values from -4 to 4, as said below
Outputs:
- dressed_real: bfloat16 [8, 96, 128, 128], P('kz', 'en')
- dressed_imag: bfloat16 [8, 96, 128, 128], P('kz', 'en')
Inputs may be any that keep to these rules, and one draw needn't show every extreme that they name: Each row of offsets holds each of -4 to -1 and 1 to 4 exactly once.
All inputs are finite; a program needn't handle non-finite values.
Results may differ from a plain program's by a relative error of at most 0.007.
Values may be sent and summed in bfloat16 or wider, within the bound.
A program may use at most 128 MiB of HBM per device.

v0:
```python
import functools

import jax
import jax.numpy as jnp
from jax import lax
from jax.experimental import pallas as pl
from jax.experimental.pallas import tpu as pltpu
from jax.sharding import PartitionSpec as P

REACH = 4
TILE = 64
SLOTS = 3
KIND = jnp.bfloat16
LANES = 16
MESH = pl.DeviceIdType.MESH


def pieces_of(energies):
    pieces = [(energies - REACH, REACH), (0, REACH)]
    while sum(size for _, size in pieces) < energies:
        start = pieces[-1][0] + pieces[-1][1]
        pieces.append((start, min(SLOTS, energies - REACH - start)))
    return pieces


def kernel(counts, real_hbm, imag_hbm, coupling, strengths, offsets, out_real, out_imag,
           own, near, far, turned, flat, weights, summed, sigma,
           own_sem, far_send, far_recv, near_send, near_recv, halo_send, halo_recv):
    momenta, sections = counts
    hops, branches, orbitals = coupling.shape[0], coupling.shape[1], coupling.shape[-1]
    energies = own.shape[1]
    pieces = pieces_of(energies)
    kz, en = lax.axis_index("kz"), lax.axis_index("en")
    odd = lax.rem(kz, 2)
    partner = kz + 1 - 2 * odd
    ahead, behind = lax.rem(kz + 2, momenta), lax.rem(kz + momenta - 2, momenta)
    has_low, has_high = en > 0, en < sections - 1
    sources = (real_hbm, imag_hbm)
    fields = (near, far)

    barrier = pltpu.get_barrier_semaphore()
    for other in (partner, ahead, behind):
        pl.semaphore_signal(barrier, inc=1, device_id=(other, en), device_id_type=MESH)

    @pl.when(has_low)
    def _():
        pl.semaphore_signal(barrier, inc=1, device_id=(kz, en - 1), device_id_type=MESH)

    @pl.when(has_high)
    def _():
        pl.semaphore_signal(barrier, inc=1, device_id=(kz, en + 1), device_id_type=MESH)

    pl.semaphore_wait(barrier, 3 + has_low.astype(jnp.int32) + has_high.astype(jnp.int32))

    def rows(piece):
        return pl.ds(REACH + pieces[piece][0], pieces[piece][1])

    def inner(piece, part):
        return sources[part].at[0, pl.ds(*pieces[piece])]

    def far_copy(chunk, part):
        return pltpu.make_async_remote_copy(
            inner(chunk, part), far.at[part, rows(chunk)],
            far_send.at[chunk, part], far_recv.at[chunk, part],
            device_id=(ahead, en), device_id_type=MESH)

    def near_copy(chunk, part, relay):
        source = far.at[part, rows(chunk)] if relay else inner(chunk, part)
        return pltpu.make_async_remote_copy(
            source, near.at[part, rows(chunk)],
            near_send.at[chunk, part], near_recv.at[chunk, part],
            device_id=(partner, en), device_id_type=MESH)

    def halo_copy(hop, side, part):
        field = fields[hop]
        if side == 0:
            source, target, to = energies, 0, lax.rem(en + 1, sections)
        else:
            source, target, to = REACH, REACH + energies, lax.rem(en + sections - 1, sections)
        return pltpu.make_async_remote_copy(
            field.at[part, pl.ds(source, REACH)], field.at[part, pl.ds(target, REACH)],
            halo_send.at[hop, side, part], halo_recv.at[hop, side, part],
            device_id=(kz, to), device_id_type=MESH)

    order = range(len(pieces))
    for chunk in order:
        for part in range(2):
            far_copy(chunk, part).start()

    @pl.when(odd == 0)
    def _():
        for chunk in order:
            for part in range(2):
                near_copy(chunk, part, False).start()

    locals_ = [pltpu.make_async_copy(sources[part].at[0], own.at[part], own_sem.at[part]) for part in range(2)]
    for copy in locals_:
        copy.start()

    zeros = jnp.zeros((2, REACH, orbitals, orbitals), jnp.bfloat16)

    @pl.when(en == 0)
    def _():
        near[:, pl.ds(0, REACH)] = zeros
        far[:, pl.ds(0, REACH)] = zeros

    @pl.when(en == sections - 1)
    def _():
        near[:, pl.ds(REACH + energies, REACH)] = zeros
        far[:, pl.ds(REACH + energies, REACH)] = zeros

    for hop in range(hops):
        for branch in range(branches):
            matrix = coupling[hop, branch, 0]
            side, other = branch % 2 * orbitals, (1 - branch % 2) * orbitals
            turned[hop, branch // 2, side:side + orbitals, side:side + orbitals] = (
                matrix.astype(jnp.float32).T.astype(jnp.bfloat16))
            turned[hop, branch // 2, side:side + orbitals, other:other + orbitals] = jnp.zeros_like(matrix)
            place = (hop * branches + branch) * orbitals
            flat[:, place:place + orbitals] = matrix
            for tap in range(2 * REACH + 1):
                if tap == REACH:
                    continue
                total = jnp.float32(0)
                for index in range(offsets.shape[1]):
                    total = total + jnp.where(
                        offsets[hop, index] == REACH - tap, strengths[hop, branch, index], 0.0)
                weights[(hop * branches + branch) * (2 * REACH + 1) + tap] = jnp.full(
                    (LANES, orbitals), total, jnp.float32).astype(KIND)
    for copy in locals_:
        copy.wait()

    def mix(energy, slot, hop, part, row):
        field = fields[hop]
        sums = [None] * branches
        for tap in range(2 * REACH + 1):
            if tap == REACH:
                continue
            window = field[part, energy + tap, row:row + TILE, :].astype(KIND)
            for branch in range(branches):
                scale = weights[(hop * branches + branch) * (2 * REACH + 1) + tap]
                term = jnp.concatenate([scale] * (TILE // LANES), axis=0) * window
                sums[branch] = term if sums[branch] is None else sums[branch] + term
        for branch in range(branches):
            side = branch % 2 * orbitals
            summed[slot, hop, branch // 2, part * orbitals + row:part * orbitals + row + TILE, side:side + orbitals] = (
                sums[branch].astype(jnp.bfloat16))

    def right(slot, hop, pair):
        both = jnp.dot(summed[slot, hop, pair], turned[hop, pair],
                       preferred_element_type=jnp.float32).astype(jnp.bfloat16)
        return [jnp.concatenate([both[:orbitals, side:side + orbitals], both[orbitals:, side:side + orbitals]], axis=1)
                for side in (0, orbitals)]

    def paired(real, imag):
        return jnp.concatenate(
            [jnp.concatenate([real, imag], axis=1), jnp.concatenate([-imag, real], axis=1)], axis=0)

    def product(energy, slot):
        real, imag = own[0, energy], own[1, energy]
        return jnp.dot(jnp.concatenate([real, imag], axis=1),
                       paired(sigma[slot, :, :orbitals], sigma[slot, :, orbitals:]),
                       preferred_element_type=jnp.float32).astype(jnp.bfloat16)

    def dress(energy, prod):
        real, imag = own[0, energy], own[1, energy]
        back = jnp.dot(prod, paired(real, imag), preferred_element_type=jnp.float32) / orbitals
        out_real[0, energy] = (real.astype(jnp.float32) + back[:, :orbitals]).astype(jnp.bfloat16)
        out_imag[0, energy] = (imag.astype(jnp.float32) + back[:, orbitals:]).astype(jnp.bfloat16)

    def stage(energy, place, mixes=True, lefts=True):
        mix_slot, left_slot, last_slot = place % SLOTS, (place - 1) % SLOTS, (place - 2) % SLOTS
        last = jnp.maximum(energy - 2, 0)
        prod = product(last, last_slot)
        parts = []
        units = [(part, row) for part in range(2) for row in range(0, orbitals, TILE)]
        share = -(-2 * len(units) // branches)
        for hop in range(hops):
            for pair in range(branches // 2):
                if lefts:
                    parts += right(left_slot, hop, pair)
                if mixes:
                    for part, row in units[pair * share:(pair + 1) * share]:
                        mix(energy, mix_slot, hop, part, row)
            if hop == 0:
                dress(last, prod)
        if lefts:
            sigma[left_slot] = jnp.dot(
                flat[...], jnp.concatenate(parts, axis=0), preferred_element_type=jnp.float32).astype(jnp.bfloat16)

    def compute(first, count):
        def body(index, carry):
            for place in range(SLOTS):
                stage(first + index * SLOTS + place, place)
            return carry

        if count == SLOTS:
            body(0, 0)
        else:
            lax.fori_loop(0, count // SLOTS, body, 0)

    def drain():
        stage(energies, 0, mixes=False)
        stage(energies + 1, 1, mixes=False, lefts=False)

    def halo_out(hop, chunk):
        for side, edge, cond in ((0, 0, has_high), (1, 1, has_low)):
            if chunk == edge:
                @pl.when(cond)
                def _(side=side):
                    for part in range(2):
                        halo_copy(hop, side, part).start()

    def halo_in(side, cond):
        @pl.when(cond)
        def _():
            for hop in range(hops):
                for part in range(2):
                    halo_copy(hop, side, part).wait_recv()

    for chunk in order:
        for part in range(2):
            far_copy(chunk, part).wait_recv()

            @pl.when(odd == 1)
            def _(part=part):
                near_copy(chunk, part, True).start()
        halo_out(1, chunk)
        for part in range(2):
            near_copy(chunk, part, False).wait_recv()
        halo_out(0, chunk)
        if chunk == 2:
            halo_in(0, has_low)
        if chunk >= 2 and pieces[chunk][1] == SLOTS:
            compute((chunk - 2) * SLOTS, SLOTS)
    halo_in(1, has_high)
    done = (energies - 2 * REACH) // SLOTS * SLOTS
    compute(done, energies - done)
    drain()

    for chunk in order:
        for part in range(2):
            far_copy(chunk, part).wait_send()
            near_copy(chunk, part, False).wait_send()
    for side, cond in ((0, has_high), (1, has_low)):
        @pl.when(cond)
        def _(side=side):
            for hop in range(hops):
                for part in range(2):
                    halo_copy(hop, side, part).wait_send()


def shards(counts, green_real, green_imag, coupling, strengths, offsets):
    energies, orbitals = green_real.shape[1], green_real.shape[2]
    hops, branches = coupling.shape[0], coupling.shape[1]
    pieces = pieces_of(energies)
    anywhere = pl.BlockSpec(memory_space=pl.ANY)
    vmem = pl.BlockSpec(memory_space=pltpu.VMEM)
    smem = pl.BlockSpec(memory_space=pltpu.SMEM)
    dma = pltpu.SemaphoreType.DMA
    chunks = len(pieces_of(energies))
    extended = (2, energies + 2 * REACH, orbitals, orbitals)
    return pl.pallas_call(
        functools.partial(kernel, counts),
        out_shape=[jax.ShapeDtypeStruct(green_real.shape, jnp.bfloat16)] * 2,
        in_specs=[anywhere, anywhere, vmem, smem, smem],
        out_specs=[vmem, vmem],
        scratch_shapes=[
            pltpu.VMEM((2, energies, orbitals, orbitals), jnp.bfloat16),
            pltpu.VMEM(extended, jnp.bfloat16),
            pltpu.VMEM(extended, jnp.bfloat16),
            pltpu.VMEM((hops, branches // 2, 2 * orbitals, 2 * orbitals), jnp.bfloat16),
            pltpu.VMEM((orbitals, hops * branches * orbitals), jnp.bfloat16),
            pltpu.VMEM((hops * branches * (2 * REACH + 1), LANES, orbitals), KIND),
            pltpu.VMEM((SLOTS, hops, branches // 2, 2 * orbitals, 2 * orbitals), jnp.bfloat16),
            pltpu.VMEM((SLOTS, orbitals, 2 * orbitals), jnp.bfloat16),
            dma((2,)),
            dma((chunks, 2)), dma((chunks, 2)),
            dma((chunks, 2)), dma((chunks, 2)),
            dma((hops, 2, 2)), dma((hops, 2, 2)),
        ],
        compiler_params=pltpu.CompilerParams(
            collective_id=0, has_side_effects=True, vmem_limit_bytes=24 * 2**20),
    )(green_real, green_imag, coupling, strengths, offsets)


def solution(mesh):
    blocks = P("kz", "en", None, None)
    counts = (mesh.shape["kz"], mesh.shape["en"])
    return jax.shard_map(
        functools.partial(shards, counts), mesh=mesh,
        in_specs=(blocks, blocks, P(None, None, "kz", None, None), P(), P()),
        out_specs=(blocks, blocks), check_vma=False)
```

profile of v0, /device:TPU:0, one launch (start us, length us, event | category | flops | bytes accessed | tf_op | source)
XLA Modules:
  0.0 61.9 jit_solution(1411918403621017796)
XLA Ops:
  0.6 0.0 copy-start
  0.6 1.1 %copy-done = bf16[1,24,128,128]{3,2,1,0:T(8,128)(2,1)S(1)} copy-done((bf16[1,24,128,128]{3,2,1,0:T(8,128)(2,1)S(1)}, bf16[1,24,128,128]{3,2,1,0:T(8,128)(2,1)}, u32[]{:S(2)}) %copy-start) | copy-done | bytes 786456
  1.8 0.0 copy-start.1
  1.8 1.1 %copy-done.1 = bf16[1,24,128,128]{3,2,1,0:T(8,128)(2,1)S(1)} copy-done((bf16[1,24,128,128]{3,2,1,0:T(8,128)(2,1)S(1)}, bf16[1,24,128,128]{3,2,1,0:T(8,128)(2,1)}, u32[]{:S(2)}) %copy-start.1) | copy-done | bytes 786456
  2.9 0.0 copy-start.2
  2.9 0.9 %copy-done.2 = bf16[2,4,1,128,128]{4,3,2,1,0:T(8,128)(2,1)S(1)} copy-done((bf16[2,4,1,128,128]{4,3,2,1,0:T(8,128)(2,1)S(1)}, bf16[2,4,1,128,128]{4,3,2,1,0:T(8,128)(2,1)}, u32[]{:S(2)}) %copy-start.2) | copy-done | bytes 262168
  3.8 0.0 copy-start.3
  3.9 0.7 %copy-done.3 = f32[2,4,8]{2,1,0:T(4,128)S(1)} copy-done((f32[2,4,8]{2,1,0:T(4,128)S(1)}, f32[2,4,8]{2,1,0:T(4,128)}, u32[]{:S(2)}) %copy-start.3) | copy-done | bytes 280
  4.5 0.0 copy-start.4
  4.5 0.7 %copy-done.4 = s32[2,8]{1,0:T(2,128)S(1)} copy-done((s32[2,8]{1,0:T(2,128)S(1)}, s32[2,8]{1,0:T(2,128)}, u32[]{:S(2)}) %copy-start.4) | copy-done | bytes 88
  5.2 54.9 %shard_map.68 = (bf16[1,24,128,128]{3,2,1,0:T(8,128)(2,1)S(1)}, bf16[1,24,128,128]{3,2,1,0:T(8,128)(2,1)S(1)}) custom-call(bf16[1,24,128,128]{3,2,1,0:T(8,128)(2,1)S(1)} %copy-done, bf16[1,24,128,128]{3,2,1,0:T(8,128)(2,1)S(1)} %copy-done.1, bf16[2,4,1,128,128]{4,3,2,1,0:T(8,128)(2,1)S(1)} %copy-done.2, f32[2,4,8]{2,1,0:T(4,128)S(1)} %copy-done.3, ...), custom_call_target="tpu_custom_call" | custom-call | tf_op jit(solution)/shard_map/pallas_call | solution.py:263
  60.2 0.9 %copy.9 = bf16[1,24,128,128]{3,2,1,0:T(8,128)(2,1)} copy(bf16[1,24,128,128]{3,2,1,0:T(8,128)(2,1)S(1)} %get-tuple-element.4) | data formatting | bytes 1572864
  61.1 0.9 %copy.10 = bf16[1,24,128,128]{3,2,1,0:T(8,128)(2,1)} copy(bf16[1,24,128,128]{3,2,1,0:T(8,128)(2,1)S(1)} %get-tuple-element.5) | data formatting | bytes 1572864
Async XLA Ops:
  0.6 1.1 %copy-start = (bf16[1,24,128,128]{3,2,1,0:T(8,128)(2,1)S(1)}, bf16[1,24,128,128]{3,2,1,0:T(8,128)(2,1)}, u32[]{:S(2)}) copy-start(bf16[1,24,128,128]{3,2,1,0:T(8,128)(2,1)} %real_hbm.1) | copy-start | bytes 2359300
  1.8 1.1 %copy-start.1 = (bf16[1,24,128,128]{3,2,1,0:T(8,128)(2,1)S(1)}, bf16[1,24,128,128]{3,2,1,0:T(8,128)(2,1)}, u32[]{:S(2)}) copy-start(bf16[1,24,128,128]{3,2,1,0:T(8,128)(2,1)} %imag_hbm.1) | copy-start | bytes 2359300
  2.9 0.9 %copy-start.2 = (bf16[2,4,1,128,128]{4,3,2,1,0:T(8,128)(2,1)S(1)}, bf16[2,4,1,128,128]{4,3,2,1,0:T(8,128)(2,1)}, u32[]{:S(2)}) copy-start(bf16[2,4,1,128,128]{4,3,2,1,0:T(8,128)(2,1)} %coupling.1) | copy-start | bytes 786436
  3.8 0.7 %copy-start.3 = (f32[2,4,8]{2,1,0:T(4,128)S(1)}, f32[2,4,8]{2,1,0:T(4,128)}, u32[]{:S(2)}) copy-start(f32[2,4,8]{2,1,0:T(4,128)} %strengths.1) | copy-start | bytes 772
  4.5 0.7 %copy-start.4 = (s32[2,8]{1,0:T(2,128)S(1)}, s32[2,8]{1,0:T(2,128)}, u32[]{:S(2)}) copy-start(s32[2,8]{1,0:T(2,128)} %offsets.1) | copy-start | bytes 196
where the time goes:
time: 62.4 us; the launch traced here: 61.9 us
  Pallas kernels  54.9 us (88%)
  local copies, waits for them, and re-layouts  6.33 us (10%)
  between operations  0.65 us (1%)
    pallas_call x1, Pallas kernels, shards(): pl.pallas_call(functools.partial(kernel, counts), out_shape=[jax.ShapeDty...  54.9 us
    unnamed x12, local copies, waits for them, and re-layouts  6.33 us

commit v1 on v0

v1 whole, which is shorter than its diff:
```python
import functools

import jax
import jax.numpy as jnp
from jax import lax
from jax.experimental import pallas as pl
from jax.experimental.pallas import tpu as pltpu
from jax.sharding import PartitionSpec as P

REACH = 4
TAPS = 2 * REACH + 1
TILE = 64
LANES = 16
SINGLES = REACH + 2
MESH = pl.DeviceIdType.MESH
GRANT = 60 * 2**20


def pieces_of(energies):
    pieces = [(energies - 4, 1), (energies - 3, 1), (energies - 2, 2), (0, 2), (2, 2)]
    edges = len(pieces)
    start, last = REACH, energies - REACH
    while start < last:
        size = 2 if last - start >= SINGLES + 2 else 1
        pieces.append((start, size))
        start += size
    return pieces, edges


def kernel(counts, real_hbm, imag_hbm, coupling_hbm, strengths_hbm, offsets_hbm, real_out, imag_out,
           own, near, far, coupling, strengths, offsets, turned, flat, weights, summed, sigma, partial, rotated, dressed,
           own_sem, small_sem, out_sem, far_send, far_recv, near_send, near_recv, halo_send, halo_recv, ack):
    momenta, sections = counts
    hops, branches, orbitals = coupling.shape[0], coupling.shape[1], coupling.shape[-1]
    energies = own.shape[1]
    pieces, edges = pieces_of(energies)
    kz, en = lax.axis_index("kz"), lax.axis_index("en")
    odd = lax.rem(kz, 2)
    even = 1 - odd
    partner = kz + 1 - 2 * odd
    ahead, behind = lax.rem(kz + 2, momenta), lax.rem(kz + momenta - 2, momenta)
    has_low, has_high = en > 0, en < sections - 1
    sources, outs, fields = (real_hbm, imag_hbm), (real_out, imag_out), (near, far)

    barrier = pltpu.get_barrier_semaphore()
    pl.semaphore_signal(barrier, inc=1, device_id=(behind, en), device_id_type=MESH)

    @pl.when(even == 1)
    def _():
        pl.semaphore_signal(barrier, inc=1, device_id=(partner, en), device_id_type=MESH)

    @pl.when(has_high)
    def _():
        pl.semaphore_signal(barrier, inc=1, device_id=(kz, en + 1), device_id_type=MESH)

    smalls = [pltpu.make_async_copy(a, b, small_sem.at[i]) for i, (a, b) in enumerate(
        ((coupling_hbm, coupling), (strengths_hbm, strengths), (offsets_hbm, offsets)))]
    for copy in smalls:
        copy.start()
    pl.semaphore_wait(barrier, 1 + odd + has_low.astype(jnp.int32))

    def far_copy(piece, start, size, part):
        return pltpu.make_async_remote_copy(
            sources[part].at[0, pl.ds(start, size)], far.at[part, pl.ds(REACH + start, size)],
            far_send.at[piece, part], far_recv.at[piece, part], device_id=(ahead, en), device_id_type=MESH)

    def near_copy(piece, start, size, part, relay):
        rows = pl.ds(REACH + start, size)
        source = far.at[part, rows] if relay else sources[part].at[0, pl.ds(start, size)]
        return pltpu.make_async_remote_copy(
            source, near.at[part, rows],
            near_send.at[piece, part], near_recv.at[piece, part], device_id=(partner, en), device_id_type=MESH)

    def halo_copy(hop, side):
        field = fields[hop]
        if side == 0:
            source, target, to = energies, 0, lax.rem(en + 1, sections)
        else:
            source, target, to = REACH, REACH + energies, lax.rem(en + sections - 1, sections)
        return pltpu.make_async_remote_copy(
            field.at[:, pl.ds(source, REACH)], field.at[:, pl.ds(target, REACH)],
            halo_send.at[hop, side], halo_recv.at[hop, side], device_id=(kz, to), device_id_type=MESH)

    for piece, (start, size) in enumerate(pieces):
        for part in range(2):
            far_copy(piece, start, size, part).start()

    @pl.when(odd == 1)
    def _():
        pl.semaphore_signal(ack.at[0], inc=1, device_id=(partner, en), device_id_type=MESH)

    @pl.when(has_low)
    def _():
        pl.semaphore_signal(ack.at[1], inc=1, device_id=(kz, en - 1), device_id_type=MESH)

    @pl.when(odd == 0)
    def _():
        pl.semaphore_wait(ack.at[0], 1)
        for piece, (start, size) in enumerate(pieces):
            for part in range(2):
                near_copy(piece, start, size, part, False).start()

    owns = [pltpu.make_async_copy(sources[part].at[0], own.at[part], own_sem.at[part]) for part in range(2)]
    for copy in owns:
        copy.start()

    @pl.when(has_high)
    def _():
        pl.semaphore_wait(ack.at[1], 1)

    def arrive(piece, start, size):
        for part in range(2):
            far_copy(piece, start, size, part).wait_recv()

            @pl.when(odd == 1)
            def _(part=part):
                near_copy(piece, start, size, part, True).start()
        for part in range(2):
            near_copy(piece, start, size, part, False).wait_recv()

    zeros = jnp.zeros((2, REACH, orbitals, orbitals), jnp.bfloat16)
    blank = jnp.zeros((orbitals, orbitals), jnp.bfloat16)

    @pl.when(en == 0)
    def _():
        near[:, pl.ds(0, REACH)] = zeros
        far[:, pl.ds(0, REACH)] = zeros

    @pl.when(en == sections - 1)
    def _():
        near[:, pl.ds(REACH + energies, REACH)] = zeros
        far[:, pl.ds(REACH + energies, REACH)] = zeros

    def place_of(hop, branch):
        return hop * branches + branch

    def prepare(hop, branch):
        matrix = coupling[hop, branch, 0].astype(jnp.float32)
        turned[hop, branch] = matrix.T.astype(jnp.bfloat16)
        flat[place_of(hop, branch)] = (matrix * (1.0 / orbitals)).astype(jnp.bfloat16)
        for tap in range(TAPS):
            if tap == REACH:
                continue
            total = jnp.float32(0)
            for index in range(offsets.shape[1]):
                total = total + jnp.where(
                    offsets[hop, index] == REACH - tap, strengths[hop, branch, index], 0.0)
            weights[place_of(hop, branch) * TAPS + tap] = jnp.full(
                (LANES, orbitals), total, jnp.float32).astype(jnp.bfloat16)

    def scale_of(hop, branch, tap, rows):
        return jnp.concatenate([weights[place_of(hop, branch) * TAPS + tap]] * (rows // LANES), axis=0)

    def mix(energy, slot, hop, part, row, taps):
        field = fields[hop]
        sums = [None] * branches
        for pair in range(0, len(taps), 2):
            some = taps[pair:pair + 2]
            windows = [field[part, energy + tap, row:row + TILE, :] for tap in some]
            for branch in range(branches):
                terms = [scale_of(hop, branch, tap, TILE) * window for tap, window in zip(some, windows)]
                term = terms[0] if len(terms) == 1 else terms[0] + terms[1]
                sums[branch] = term if sums[branch] is None else sums[branch] + term
        for branch in range(branches):
            summed[slot, hop, branch, part * orbitals + row:part * orbitals + row + TILE, :] = sums[branch]

    every = [tap for tap in range(TAPS) if tap != REACH]
    units = [(part, row) for part in range(2) for row in range(0, orbitals, TILE)]
    share = -(-2 * len(units) // branches)

    def right(slot, hop, pair):
        first, second = 2 * pair, 2 * pair + 1
        both = jnp.concatenate([summed[slot, hop, first], summed[slot, hop, second]], axis=1)
        blocks = jnp.concatenate([jnp.concatenate([turned[hop, first], blank], axis=1),
                                  jnp.concatenate([blank, turned[hop, second]], axis=1)], axis=0)
        both = jnp.dot(both, blocks, preferred_element_type=jnp.float32).astype(jnp.bfloat16)
        return [jnp.concatenate([both[:orbitals, side:side + orbitals], both[orbitals:, side:side + orbitals]], axis=1)
                for side in (0, orbitals)]

    def left(parts):
        total = jnp.dot(jnp.concatenate([flat[place] for place in range(hops * branches)], axis=1),
                        jnp.concatenate(parts, axis=0), preferred_element_type=jnp.float32).astype(jnp.bfloat16)
        return total[:, :orbitals], total[:, orbitals:]

    def paired(real, imag):
        return jnp.concatenate(
            [jnp.concatenate([real, imag], axis=1), jnp.concatenate([-imag, real], axis=1)], axis=0)

    def product(energy, real, imag):
        return jnp.dot(jnp.concatenate([own[0, energy], own[1, energy]], axis=1), paired(real, imag),
                       preferred_element_type=jnp.float32).astype(jnp.bfloat16)

    def dress(energy, prod):
        real, imag = own[0, energy], own[1, energy]
        back = jnp.dot(prod, paired(real, imag), preferred_element_type=jnp.float32)
        dressed[0, energy] = (real.astype(jnp.float32) + back[:, :orbitals]).astype(jnp.bfloat16)
        dressed[1, energy] = (imag.astype(jnp.float32) + back[:, orbitals:]).astype(jnp.bfloat16)

    def stage(mixing, lefting, dressing):
        prod = None
        if dressing is not None:
            prod = product(dressing[0], sigma[dressing[1], 0], sigma[dressing[1], 1])
        parts = []
        for hop in range(hops):
            for pair in range(branches // 2):
                if lefting is not None:
                    parts += right(lefting[1], hop, pair)
                if mixing is not None:
                    for part, row in units[pair * share:(pair + 1) * share]:
                        mix(mixing[0], mixing[1], hop, part, row, every)
            if hop == 0 and prod is not None:
                dress(dressing[0], prod)
        if lefting is not None:
            real, imag = left(parts)
            sigma[lefting[1], 0], sigma[lefting[1], 1] = real, imag

    last = energies - REACH - 1
    tail = [e for e in range(last - REACH, energies) if e != last]

    def begin(energy, until, slot):
        taps = [tap for tap in every if not until < energy + tap - REACH <= last]
        for hop in range(hops):
            for part, row in units:
                mix(energy, slot, hop, part, row, taps)
        for hop in range(hops):
            for pair in range(branches // 2):
                for branch, value in zip((2 * pair, 2 * pair + 1), right(slot, hop, pair)):
                    for part in range(2):
                        partial[tail.index(energy), place_of(hop, branch), part] = (
                            value[:, part * orbitals:(part + 1) * orbitals])

    def rotate(source, hop):
        rows = jnp.concatenate([fields[hop][0, REACH + source], fields[hop][1, REACH + source]], axis=0)
        for pair in range(branches // 2):
            first, second = 2 * pair, 2 * pair + 1
            both = jnp.dot(rows, jnp.concatenate([turned[hop, first], turned[hop, second]], axis=1),
                           preferred_element_type=jnp.float32).astype(jnp.bfloat16)
            for index, branch in enumerate((first, second)):
                for part in range(2):
                    rotated[source % 2, place_of(hop, branch), part] = both[
                        part * orbitals:(part + 1) * orbitals, index * orbitals:(index + 1) * orbitals]

    def updated(energy, source, hop, branch, part):
        place = place_of(hop, branch)
        return (partial[tail.index(energy), place, part]
                + scale_of(hop, branch, source - energy + REACH, orbitals) * rotated[source % 2, place, part])

    def update(energy, source):
        for hop in range(hops):
            for branch in range(branches):
                for part in range(2):
                    partial[tail.index(energy), place_of(hop, branch), part] = updated(energy, source, hop, branch, part)

    def out_copy(index, start, size, part):
        return pltpu.make_async_copy(dressed.at[part, pl.ds(start, size)], outs[part].at[0, pl.ds(start, size)],
                                     out_sem.at[index, part])

    def out(start, size):
        for part in range(2):
            out_copy(start, start, size, part).start()

    def halo_out(hop, side, cond):
        @pl.when(cond)
        def _():
            halo_copy(hop, side).start()

    def halo_in(side, cond):
        @pl.when(cond)
        def _():
            for hop in range(hops):
                halo_copy(hop, side).wait_recv()

    jobs = [(hop, branch) for hop in range(hops) for branch in range(branches)]
    for piece in range(edges):
        arrive(piece, *pieces[piece])
        if piece == 2:
            for hop in range(hops):
                halo_out(hop, 0, has_high)
        if piece == edges - 1:
            for hop in range(hops):
                halo_out(hop, 1, has_low)
        if piece == 0:
            for copy in smalls:
                copy.wait()
        for job in jobs[piece * 2:piece * 2 + 2]:
            prepare(*job)
    for copy in owns:
        copy.wait()

    piece, start = edges, REACH
    stages = 0

    def step(energy):
        stage((energy, energy % 2), (energy - 1, (energy - 1) % 2) if energy > 0 else None,
              (energy - 2, energy % 2) if energy > 1 else None)

    halo_in(0, has_low)
    arrive(piece, *pieces[piece])
    for energy in range(pieces[piece][1]):
        step(energy)
        stages += 1
    start, piece = start + pieces[piece][1], piece + 1
    halo_in(1, has_high)
    for index, energy in enumerate(range(last + 1, energies)):
        begin(energy, last - REACH, 2 + index % 2)
    if stages == 1:
        arrive(piece, *pieces[piece])
        for energy in range(stages, stages + pieces[piece][1]):
            step(energy)
        stages += pieces[piece][1]
        start, piece = start + pieces[piece][1], piece + 1

    pairs = sum(size == 2 for _, size in pieces[piece:])
    base_piece, base_start, parity = piece, start, stages % 2

    def body(index, carry):
        first = base_start + 2 * index
        arrive(base_piece + index, first, 2)
        for offset in range(2):
            energy, slot = first - REACH + offset, (parity + offset) % 2
            stage((energy, slot), (energy - 1, 1 - slot), (energy - 2, slot))
        for part in range(2):
            out_copy(first - REACH - 2, first - REACH - 2, 2, part).start()
        return carry

    lax.fori_loop(0, pairs, body, 0)
    outs_started = [(stages - 2 + 2 * index, 2) for index in range(pairs)]
    piece, start, stages = piece + pairs, start + 2 * pairs, stages + 2 * pairs

    def late(source):
        for hop in range(hops):
            rotate(source, hop)
        for energy in tail:
            ready = last - REACH if energy > last else energy - 1
            if energy != source and abs(energy - source) <= REACH and source > ready:
                update(energy, source)

    for source in range(start, last):
        arrive(piece, source, 1)
        step(stages)
        opened = source + 1
        if last - REACH <= opened < last:
            begin(opened, source, 2)
        if source > last - REACH:
            late(source)
        out(stages - 2, 1)
        outs_started.append((stages - 2, 1))
        stages += 1
        piece += 1
    before = stages - 1
    stage((last, stages % 2), (before, before % 2), (before - 1, (before - 1) % 2))
    out(before - 1, 1)
    stage(None, (last, stages % 2), (before, before % 2))
    out(before, 1)
    outs_started += [(before - 1, 1), (before, 1)]

    def sends(wanted):
        for index in wanted:
            for part in range(2):
                far_copy(index, *pieces[index], part).wait_send()
                near_copy(index, *pieces[index], part, False).wait_send()

    arrive(piece, last, 1)
    for hop in range(hops):
        rotate(last, hop)
    waiting = [(last, product(last, sigma[stages % 2, 0], sigma[stages % 2, 1]))]
    sums = []
    for energy in tail + [None, None]:
        made = None
        if energy is not None:
            parts = [jnp.concatenate([updated(energy, last, hop, branch, part) for part in range(2)], axis=1)
                     for hop, branch in jobs]
            made = (energy, *left(parts))
        ready = waiting.pop(0) if waiting else None
        if sums:
            done = sums.pop(0)
            waiting.append((done[0], product(*done)))
        if made is not None:
            sums.append(made)
        if ready is not None:
            dress(*ready)
            out(ready[0], 1)
            outs_started.append((ready[0], 1))
    for ready in waiting:
        dress(*ready)
        out(ready[0], 1)
        outs_started.append((ready[0], 1))

    sends(range(len(pieces)))
    for side, cond in ((0, has_high), (1, has_low)):
        @pl.when(cond)
        def _(side=side):
            for hop in range(hops):
                halo_copy(hop, side).wait_send()
    for first, size in outs_started:
        for part in range(2):
            out_copy(first, first, size, part).wait()


def deliver(real_in, imag_in, real_out, imag_out, held, in_sem, out_sem):
    chunks = held.shape[1]
    size = held.shape[2]
    refs = ((real_in, real_out), (imag_in, imag_out))

    def fetch(part, chunk):
        return pltpu.make_async_copy(
            refs[part][0].at[0, pl.ds(chunk * size, size)], held.at[part, chunk], in_sem.at[part, chunk])

    def store(part, chunk):
        return pltpu.make_async_copy(
            held.at[part, chunk], refs[part][1].at[0, pl.ds(chunk * size, size)], out_sem.at[part, chunk])

    order = [(part, chunk) for chunk in range(chunks) for part in range(2)]
    for key in order:
        fetch(*key).start()
    for key in order:
        fetch(*key).wait()
        store(*key).start()
    for key in order:
        store(*key).wait()


def shards(counts, green_real, green_imag, coupling, strengths, offsets):
    energies, orbitals = green_real.shape[1], green_real.shape[2]
    hops, branches = coupling.shape[0], coupling.shape[1]
    pieces, _ = pieces_of(energies)
    anywhere = pl.BlockSpec(memory_space=pl.ANY)
    dma = pltpu.SemaphoreType.DMA
    chunks = len(pieces)
    square = (orbitals, orbitals)
    extended = (2, energies + 2 * REACH) + square
    shapes = [jax.ShapeDtypeStruct(green_real.shape, jnp.bfloat16)] * 2
    dressed = pl.pallas_call(
        functools.partial(kernel, counts),
        out_shape=shapes,
        in_specs=[anywhere] * 5,
        out_specs=[anywhere] * 2,
        scratch_shapes=[
            pltpu.VMEM((2, energies) + square, jnp.bfloat16),
            pltpu.VMEM(extended, jnp.bfloat16),
            pltpu.VMEM(extended, jnp.bfloat16),
            pltpu.VMEM(coupling.shape, jnp.bfloat16),
            pltpu.SMEM(strengths.shape, jnp.float32),
            pltpu.SMEM(offsets.shape, jnp.int32),
            pltpu.VMEM((hops, branches) + square, jnp.bfloat16),
            pltpu.VMEM((hops * branches,) + square, jnp.bfloat16),
            pltpu.VMEM((hops * branches * TAPS, LANES, orbitals), jnp.bfloat16),
            pltpu.VMEM((4, hops, branches, 2 * orbitals, orbitals), jnp.bfloat16),
            pltpu.VMEM((2, 2) + square, jnp.bfloat16),
            pltpu.VMEM((2 * REACH, hops * branches, 2) + square, jnp.bfloat16),
            pltpu.VMEM((2, hops * branches, 2) + square, jnp.bfloat16),
            pltpu.VMEM((2, energies) + square, jnp.bfloat16),
            dma((2,)), dma((3,)), dma((energies, 2)),
            dma((chunks, 2)), dma((chunks, 2)),
            dma((chunks, 2)), dma((chunks, 2)),
            dma((hops, 2)), dma((hops, 2)),
            pltpu.SemaphoreType.REGULAR((2,)),
        ],
        compiler_params=pltpu.CompilerParams(
            collective_id=0, has_side_effects=True, vmem_limit_bytes=GRANT),
    )(green_real, green_imag, coupling, strengths, offsets)
    parts = 3 if energies % 3 == 0 else 1
    return pl.pallas_call(
        deliver,
        out_shape=shapes,
        in_specs=[anywhere] * 2,
        out_specs=[anywhere] * 2,
        scratch_shapes=[
            pltpu.VMEM((2, parts, energies // parts) + square, jnp.bfloat16),
            dma((2, parts)), dma((2, parts)),
        ],
        compiler_params=pltpu.CompilerParams(vmem_limit_bytes=GRANT),
    )(*dressed)


def solution(mesh):
    blocks = P("kz", "en", None, None)
    counts = (mesh.shape["kz"], mesh.shape["en"])
    return jax.shard_map(
        functools.partial(shards, counts), mesh=mesh,
        in_specs=(blocks, blocks, P(None, None, "kz", None, None), P(), P()),
        out_specs=(blocks, blocks), check_vma=False)
```

time: 62.4 us -> 58.8 us (0.942)
  the two profiles are of different devices: /device:TPU:0 before, /device:TPU:1 now
where the time goes in v1:
time: 58.8 us; the launch traced here: 58.7 us
  Pallas kernels  57.9 us (98%)
  between operations  0.8 us (1%)
    pallas_call x1, Pallas kernels, shards(): pl.pallas_call(functools.partial(kernel, counts), out_shape=shapes, in_sp...  55.7 us
    pallas_call x1, Pallas kernels, shards(): pl.pallas_call(deliver, out_shape=shapes, in_specs=[anywhere] * 2, out_sp...  2.19 us

profile of v1, /device:TPU:1, one launch (start us, length us, event | category | flops | bytes accessed | tf_op | source)
XLA Modules:
  0.0 58.7 jit_solution(12779681901377484916)
XLA Ops:
  0.6 55.7 %shard_map.68 = (bf16[1,24,128,128]{3,2,1,0:T(8,128)(2,1)}, bf16[1,24,128,128]{3,2,1,0:T(8,128)(2,1)}) custom-call(bf16[1,24,128,128]{3,2,1,0:T(8,128)(2,1)} %real_hbm.1, bf16[1,24,128,128]{3,2,1,0:T(8,128)(2,1)} %imag_hbm.1, bf16[2,4,1,128,128]{4,3,2,1,0:T(8,128)(2,1)} %coupling_hbm.1, f32[2,4,8]{2,1,0:T(4,128)} %strengths_hbm.1, s32[2,8]{1,0:T(2,128)} %offsets_hbm.1), custom_call_target="tpu_custom_call" | custom-call | tf_op jit(solution)/shard_map/pallas_call | solution.py:433
  56.3 2.2 %shard_map.69 = (bf16[1,24,128,128]{3,2,1,0:T(8,128)(2,1)}, bf16[1,24,128,128]{3,2,1,0:T(8,128)(2,1)}) custom-call(bf16[1,24,128,128]{3,2,1,0:T(8,128)(2,1)} %get-tuple-element.4.real_in, bf16[1,24,128,128]{3,2,1,0:T(8,128)(2,1)} %get-tuple-element.5.imag_in), custom_call_target="tpu_custom_call" | custom-call | tf_op jit(solution)/shard_map/pallas_call | solution.py:463

commit v2 on v1

v2 whole, which is shorter than its diff:
```python
import functools

import jax
import jax.numpy as jnp
from jax import lax
from jax.experimental import pallas as pl
from jax.experimental.pallas import tpu as pltpu
from jax.sharding import PartitionSpec as P

REACH = 4
TAPS = 2 * REACH + 1
TILE = 64
LANES = 16
MESH = pl.DeviceIdType.MESH
GRANT = 60 * 2**20


def pieces_of(energies):
    order = list(range(energies - REACH, energies)) + list(range(energies - REACH))
    pieces = [(energy, 1) for energy in order]
    edges = 2 * REACH
    return pieces, edges


def kernel(counts, real_hbm, imag_hbm, coupling_hbm, strengths_hbm, offsets_hbm, real_out, imag_out,
           own, near, far, coupling, strengths, offsets, turned, flat, weights, sigma, partial, rotated, dressed,
           own_sem, small_sem, out_sem, far_send, far_recv, near_send, near_recv, halo_send, halo_recv, ack):
    momenta, sections = counts
    hops, branches, orbitals = coupling.shape[0], coupling.shape[1], coupling.shape[-1]
    energies = own.shape[1]
    pieces, edges = pieces_of(energies)
    kz, en = lax.axis_index("kz"), lax.axis_index("en")
    odd = lax.rem(kz, 2)
    even = 1 - odd
    partner = kz + 1 - 2 * odd
    ahead, behind = lax.rem(kz + 2, momenta), lax.rem(kz + momenta - 2, momenta)
    has_low, has_high = en > 0, en < sections - 1
    sources, outs, fields = (real_hbm, imag_hbm), (real_out, imag_out), (near, far)

    barrier = pltpu.get_barrier_semaphore()
    pl.semaphore_signal(barrier, inc=1, device_id=(behind, en), device_id_type=MESH)

    @pl.when(even == 1)
    def _():
        pl.semaphore_signal(barrier, inc=1, device_id=(partner, en), device_id_type=MESH)

    @pl.when(has_high)
    def _():
        pl.semaphore_signal(barrier, inc=1, device_id=(kz, en + 1), device_id_type=MESH)

    smalls = [pltpu.make_async_copy(a, b, small_sem.at[i]) for i, (a, b) in enumerate(
        ((coupling_hbm, coupling), (strengths_hbm, strengths), (offsets_hbm, offsets)))]
    for copy in smalls:
        copy.start()
    pl.semaphore_wait(barrier, 1 + odd + has_low.astype(jnp.int32))

    def far_copy(piece, start, size, part):
        return pltpu.make_async_remote_copy(
            sources[part].at[0, pl.ds(start, size)], far.at[part, pl.ds(REACH + start, size)],
            far_send.at[part], far_recv.at[piece, part], device_id=(ahead, en), device_id_type=MESH)

    def near_copy(piece, start, size, part, relay):
        rows = pl.ds(REACH + start, size)
        source = far.at[part, rows] if relay else sources[part].at[0, pl.ds(start, size)]
        return pltpu.make_async_remote_copy(
            source, near.at[part, rows],
            near_send.at[part], near_recv.at[piece], device_id=(partner, en), device_id_type=MESH)

    def halo_copy(hop, side):
        field = fields[hop]
        if side == 0:
            source, target, to = energies, 0, lax.rem(en + 1, sections)
        else:
            source, target, to = REACH, REACH + energies, lax.rem(en + sections - 1, sections)
        return pltpu.make_async_remote_copy(
            field.at[:, pl.ds(source, REACH)], field.at[:, pl.ds(target, REACH)],
            halo_send.at[hop, side], halo_recv.at[hop, side], device_id=(kz, to), device_id_type=MESH)

    @pl.when(odd == 1)
    def _():
        pl.semaphore_signal(ack.at[0], inc=1, device_id=(partner, en), device_id_type=MESH)

    @pl.when(has_low)
    def _():
        pl.semaphore_signal(ack.at[1], inc=1, device_id=(kz, en - 1), device_id_type=MESH)

    def send_far(first, stop):
        for piece in range(first, stop):
            for part in range(2):
                far_copy(piece, *pieces[piece], part).start()

    def send_near(first, stop):
        @pl.when(odd == 0)
        def _():
            if first == 0:
                pl.semaphore_wait(ack.at[0], 1)
            for piece in range(first, stop):
                for part in range(2):
                    near_copy(piece, *pieces[piece], part, False).start()

    send_far(0, edges)
    send_near(0, edges)
    send_far(edges, len(pieces))
    send_near(edges, len(pieces))

    owns = [pltpu.make_async_copy(sources[part].at[0], own.at[part], own_sem.at[part]) for part in range(2)]
    for copy in owns:
        copy.start()

    @pl.when(has_high)
    def _():
        pl.semaphore_wait(ack.at[1], 1)

    def arrive(piece, start, size):
        for part in range(2):
            far_copy(piece, start, size, part).wait_recv()

            @pl.when(odd == 1)
            def _(part=part):
                near_copy(piece, start, size, part, True).start()
        rows = pl.ds(REACH + start, size)
        pltpu.make_async_copy(near.at[:, rows], near.at[:, rows], near_recv.at[piece]).wait()

    zeros = jnp.zeros((2, REACH, orbitals, orbitals), jnp.bfloat16)
    blank = jnp.zeros((orbitals, orbitals), jnp.bfloat16)

    @pl.when(en == 0)
    def _():
        near[:, pl.ds(0, REACH)] = zeros
        far[:, pl.ds(0, REACH)] = zeros

    @pl.when(en == sections - 1)
    def _():
        near[:, pl.ds(REACH + energies, REACH)] = zeros
        far[:, pl.ds(REACH + energies, REACH)] = zeros

    def place_of(hop, branch):
        return hop * branches + branch

    def prepare(hop, branch):
        matrix = coupling[hop, branch, 0].astype(jnp.float32)
        turned[hop, branch] = matrix.T.astype(jnp.bfloat16)
        flat[place_of(hop, branch)] = (matrix * (1.0 / orbitals)).astype(jnp.bfloat16)
        for tap in range(TAPS):
            if tap == REACH:
                continue
            total = jnp.float32(0)
            for index in range(offsets.shape[1]):
                total = total + jnp.where(
                    offsets[hop, index] == REACH - tap, strengths[hop, branch, index], 0.0)
            weights[place_of(hop, branch) * TAPS + tap] = jnp.full(
                (LANES, orbitals), total, jnp.float32).astype(jnp.bfloat16)

    def scale_of(hop, branch, tap, rows):
        return jnp.concatenate([weights[place_of(hop, branch) * TAPS + tap]] * (rows // LANES), axis=0)

    every = [tap for tap in range(TAPS) if tap != REACH]

    def right(energy, hop, pair, taps):
        field = fields[hop]
        both = (2 * pair, 2 * pair + 1)
        rows = []
        for part in range(2):
            for row in range(0, orbitals, TILE):
                sums = [None, None]
                for first in range(0, len(taps), 2):
                    some = taps[first:first + 2]
                    windows = [field[part, energy + tap, row:row + TILE, :] for tap in some]
                    for index, branch in enumerate(both):
                        terms = [scale_of(hop, branch, tap, TILE) * window for tap, window in zip(some, windows)]
                        term = terms[0] if len(terms) == 1 else terms[0] + terms[1]
                        sums[index] = term if sums[index] is None else sums[index] + term
                rows.append(jnp.concatenate(sums, axis=1))
        blocks = jnp.concatenate([jnp.concatenate([turned[hop, both[0]], blank], axis=1),
                                  jnp.concatenate([blank, turned[hop, both[1]]], axis=1)], axis=0)
        made = jnp.dot(jnp.concatenate(rows, axis=0), blocks, preferred_element_type=jnp.float32).astype(jnp.bfloat16)
        return [jnp.concatenate([made[:orbitals, side:side + orbitals], made[orbitals:, side:side + orbitals]], axis=1)
                for side in (0, orbitals)]

    def left(parts):
        total = jnp.dot(jnp.concatenate([flat[place] for place in range(hops * branches)], axis=1),
                        jnp.concatenate(parts, axis=0), preferred_element_type=jnp.float32).astype(jnp.bfloat16)
        return total[:, :orbitals], total[:, orbitals:]

    def paired(real, imag):
        return jnp.concatenate(
            [jnp.concatenate([real, imag], axis=1), jnp.concatenate([-imag, real], axis=1)], axis=0)

    def product(energy, real, imag):
        return jnp.dot(jnp.concatenate([own[0, energy], own[1, energy]], axis=1), paired(real, imag),
                       preferred_element_type=jnp.float32).astype(jnp.bfloat16)

    def dress(energy, prod):
        real, imag = own[0, energy], own[1, energy]
        back = jnp.dot(prod, paired(real, imag), preferred_element_type=jnp.float32)
        dressed[0, energy] = (real.astype(jnp.float32) + back[:, :orbitals]).astype(jnp.bfloat16)
        dressed[1, energy] = (imag.astype(jnp.float32) + back[:, orbitals:]).astype(jnp.bfloat16)

    def stage(energy, slot, before):
        if before is not None:
            prod = product(before, sigma[1 - slot, 0], sigma[1 - slot, 1])
        parts = []
        for hop in range(hops):
            for pair in range(branches // 2):
                parts += right(energy, hop, pair, every)
            if hop == 0 and before is not None:
                dress(before, prod)
        sigma[slot, 0], sigma[slot, 1] = left(parts)

    last = energies - REACH - 1
    tail = [e for e in range(last - REACH, energies) if e != last]

    def begin(energy, until):
        taps = [tap for tap in every if not until < energy + tap - REACH <= last]
        for hop in range(hops):
            for pair in range(branches // 2):
                for branch, value in zip((2 * pair, 2 * pair + 1), right(energy, hop, pair, taps)):
                    for part in range(2):
                        partial[tail.index(energy), place_of(hop, branch), part] = (
                            value[:, part * orbitals:(part + 1) * orbitals])

    def ready(energy):
        return last - REACH if energy > last else energy - 1

    def rotate(source, hop):
        rows = jnp.concatenate([fields[hop][0, REACH + source], fields[hop][1, REACH + source]], axis=0)
        for pair in range(branches // 2):
            first, second = 2 * pair, 2 * pair + 1
            both = jnp.dot(rows, jnp.concatenate([turned[hop, first], turned[hop, second]], axis=1),
                           preferred_element_type=jnp.float32).astype(jnp.bfloat16)
            for index, branch in enumerate((first, second)):
                for part in range(2):
                    rotated[last - source, place_of(hop, branch), part] = both[
                        part * orbitals:(part + 1) * orbitals, index * orbitals:(index + 1) * orbitals]

    def updated(energy, hop, branch, part):
        place = place_of(hop, branch)
        total = None
        for source in range(last - REACH + 1, last + 1):
            if source > ready(energy) and source != energy and abs(source - energy) <= REACH:
                term = scale_of(hop, branch, source - energy + REACH, orbitals) * rotated[last - source, place, part]
                total = term if total is None else total + term
        return total + partial[tail.index(energy), place, part]

    def out_copy(start, size, part):
        return pltpu.make_async_copy(
            dressed.at[part, pl.ds(start, size)], outs[part].at[0, pl.ds(start, size)], out_sem.at[part])

    def out(start, size):
        for part in range(2):
            out_copy(start, size, part).start()

    def halo_out(hop, side, cond):
        @pl.when(cond)
        def _():
            halo_copy(hop, side).start()

    def halo_in(side, cond):
        @pl.when(cond)
        def _():
            for hop in range(hops):
                halo_copy(hop, side).wait_recv()

    jobs = [(hop, branch) for hop in range(hops) for branch in range(branches)]
    for piece in range(edges):
        arrive(piece, *pieces[piece])
        if piece == REACH - 1:
            for hop in range(hops):
                halo_out(hop, 0, has_high)
        if piece == edges - 1:
            for hop in range(hops):
                halo_out(hop, 1, has_low)
        if piece == 0:
            for copy in smalls:
                copy.wait()
        for job in jobs[piece::edges]:
            prepare(*job)
    for copy in owns:
        copy.wait()

    piece, start = edges, REACH
    stages = 0

    def step(energy):
        stage(energy, energy % 2, energy - 1 if energy > 0 else None)

    halo_in(0, has_low)
    count = last - 1 - 2 * REACH
    for energy in range(2 - count % 2):
        arrive(piece, *pieces[piece])
        step(energy)
        stages, start, piece = stages + 1, start + 1, piece + 1
    pairs = (count - stages) // 2
    if stages > 1:
        out(0, stages - 1)

    base_piece, base_start, parity = piece, start, stages % 2

    def body(index, carry):
        first = base_start + 2 * index
        for offset in range(2):
            arrive(base_piece + 2 * index + offset, first + offset, 1)
            energy = first - REACH + offset
            stage(energy, (parity + offset) % 2, energy - 1)
        for part in range(2):
            out_copy(first - REACH - 1, 2, part).start()
        return carry

    split = pairs - 1
    lax.fori_loop(0, split, body, 0)
    halo_in(1, has_high)
    upper = list(range(last + 1, energies))
    for energy in upper[:2]:
        begin(energy, last - REACH)
    lax.fori_loop(split, pairs, body, 0)
    for energy in upper[2:]:
        begin(energy, last - REACH)
    piece, start, stages = piece + 2 * pairs, start + 2 * pairs, stages + 2 * pairs

    for source in range(start, last):
        arrive(piece, source, 1)
        step(stages)
        opened = source + 1
        if last - REACH <= opened < last:
            begin(opened, source)
        if source > last - REACH:
            for hop in range(hops):
                rotate(source, hop)
        out(stages - 1, 1)
        stages += 1
        piece += 1
    stage(last, stages % 2, stages - 1)
    out(stages - 1, 1)

    for side, cond in ((0, has_high), (1, has_low)):
        @pl.when(cond)
        def _(side=side):
            for hop in range(hops):
                halo_copy(hop, side).wait_send()
    arrive(piece, last, 1)
    for hop in range(hops):
        rotate(last, hop)
    waiting = [(last, product(last, sigma[stages % 2, 0], sigma[stages % 2, 1]))]
    sums = []
    for energy in tail + [None, None]:
        made = None
        if energy is not None:
            parts = [jnp.concatenate([updated(energy, hop, branch, part) for part in range(2)], axis=1)
                     for hop, branch in jobs]
            made = (energy, *left(parts))
        turn = waiting.pop(0) if waiting else None
        if sums:
            done = sums.pop(0)
            waiting.append((done[0], product(*done)))
        if made is not None:
            sums.append(made)
        if turn is not None:
            dress(*turn)
            out(turn[0], 1)

    for part in range(2):
        far_copy(0, 0, energies, part).wait_send()
        near_copy(0, 0, energies, part, False).wait_send()
        out_copy(0, energies, part).wait()


def deliver(real_in, imag_in, real_out, imag_out, held, in_sem, out_sem):
    chunks = held.shape[1]
    size = held.shape[2]
    refs = ((real_in, real_out), (imag_in, imag_out))

    def fetch(part, chunk):
        return pltpu.make_async_copy(
            refs[part][0].at[0, pl.ds(chunk * size, size)], held.at[part, chunk], in_sem.at[part, chunk])

    def store(part, chunk):
        return pltpu.make_async_copy(
            held.at[part, chunk], refs[part][1].at[0, pl.ds(chunk * size, size)], out_sem.at[part, chunk])

    order = [(part, chunk) for chunk in range(chunks) for part in range(2)]
    for key in order:
        fetch(*key).start()
    for key in order:
        fetch(*key).wait()
        store(*key).start()
    for key in order:
        store(*key).wait()


def shards(counts, green_real, green_imag, coupling, strengths, offsets):
    energies, orbitals = green_real.shape[1], green_real.shape[2]
    hops, branches = coupling.shape[0], coupling.shape[1]
    pieces, _ = pieces_of(energies)
    anywhere = pl.BlockSpec(memory_space=pl.ANY)
    dma = pltpu.SemaphoreType.DMA
    chunks = len(pieces)
    square = (orbitals, orbitals)
    extended = (2, energies + 2 * REACH) + square
    shapes = [jax.ShapeDtypeStruct(green_real.shape, jnp.bfloat16)] * 2
    dressed = pl.pallas_call(
        functools.partial(kernel, counts),
        out_shape=shapes,
        in_specs=[anywhere] * 5,
        out_specs=[anywhere] * 2,
        scratch_shapes=[
            pltpu.VMEM((2, energies) + square, jnp.bfloat16),
            pltpu.VMEM(extended, jnp.bfloat16),
            pltpu.VMEM(extended, jnp.bfloat16),
            pltpu.VMEM(coupling.shape, jnp.bfloat16),
            pltpu.SMEM(strengths.shape, jnp.float32),
            pltpu.SMEM(offsets.shape, jnp.int32),
            pltpu.VMEM((hops, branches) + square, jnp.bfloat16),
            pltpu.VMEM((hops * branches,) + square, jnp.bfloat16),
            pltpu.VMEM((hops * branches * TAPS, LANES, orbitals), jnp.bfloat16),
            pltpu.VMEM((2, 2) + square, jnp.bfloat16),
            pltpu.VMEM((2 * REACH, hops * branches, 2) + square, jnp.bfloat16),
            pltpu.VMEM((REACH, hops * branches, 2) + square, jnp.bfloat16),
            pltpu.VMEM((2, energies) + square, jnp.bfloat16),
            dma((2,)), dma((3,)), dma((2,)),
            dma((2,)), dma((chunks, 2)),
            dma((2,)), dma((chunks,)),
            dma((hops, 2)), dma((hops, 2)),
            pltpu.SemaphoreType.REGULAR((2,)),
        ],
        compiler_params=pltpu.CompilerParams(
            collective_id=0, has_side_effects=True, vmem_limit_bytes=GRANT),
    )(green_real, green_imag, coupling, strengths, offsets)
    parts = 3 if energies % 3 == 0 else 1
    return pl.pallas_call(
        deliver,
        out_shape=shapes,
        in_specs=[anywhere] * 2,
        out_specs=[anywhere] * 2,
        scratch_shapes=[
            pltpu.VMEM((2, parts, energies // parts) + square, jnp.bfloat16),
            dma((2, parts)), dma((2, parts)),
        ],
        compiler_params=pltpu.CompilerParams(vmem_limit_bytes=GRANT),
    )(*dressed)


def solution(mesh):
    blocks = P("kz", "en", None, None)
    counts = (mesh.shape["kz"], mesh.shape["en"])
    return jax.shard_map(
        functools.partial(shards, counts), mesh=mesh,
        in_specs=(blocks, blocks, P(None, None, "kz", None, None), P(), P()),
        out_specs=(blocks, blocks), check_vma=False)
```

time: 58.8 us -> 51.6 us (0.88)
  the two profiles are of different devices: /device:TPU:1 before, /device:TPU:0 now
where the time goes in v2:
time: 51.6 us; the launch traced here: 51.4 us
  Pallas kernels  50.8 us (98%)
  between operations  0.64 us (1%)
    pallas_call x1, Pallas kernels, shards(): pl.pallas_call(functools.partial(kernel, counts), out_shape=shapes, in_sp...  48.6 us
    pallas_call x1, Pallas kernels, shards(): pl.pallas_call(deliver, out_shape=shapes, in_specs=[anywhere] * 2, out_sp...  2.19 us

profile of v2, /device:TPU:0, one launch (start us, length us, event | category | flops | bytes accessed | tf_op | source)
XLA Modules:
  0.0 51.4 jit_solution(5105658257094382723)
XLA Ops:
  0.6 48.6 %shard_map.68 = (bf16[1,24,128,128]{3,2,1,0:T(8,128)(2,1)}, bf16[1,24,128,128]{3,2,1,0:T(8,128)(2,1)}) custom-call(bf16[1,24,128,128]{3,2,1,0:T(8,128)(2,1)} %real_hbm.1, bf16[1,24,128,128]{3,2,1,0:T(8,128)(2,1)} %imag_hbm.1, bf16[2,4,1,128,128]{4,3,2,1,0:T(8,128)(2,1)} %coupling_hbm.1, f32[2,4,8]{2,1,0:T(4,128)} %strengths_hbm.1, s32[2,8]{1,0:T(2,128)} %offsets_hbm.1), custom_call_target="tpu_custom_call" | custom-call | tf_op jit(solution)/shard_map/pallas_call | solution.py:400
  49.2 2.2 %shard_map.69 = (bf16[1,24,128,128]{3,2,1,0:T(8,128)(2,1)}, bf16[1,24,128,128]{3,2,1,0:T(8,128)(2,1)}) custom-call(bf16[1,24,128,128]{3,2,1,0:T(8,128)(2,1)} %get-tuple-element.4.real_in, bf16[1,24,128,128]{3,2,1,0:T(8,128)(2,1)} %get-tuple-element.5.imag_in), custom_call_target="tpu_custom_call" | custom-call | tf_op jit(solution)/shard_map/pallas_call | solution.py:429

commit v3 on v2

--- a/solution.py
+++ b/solution.py
@@ -11,6 +11,7 @@
 TAPS = 2 * REACH + 1
 TILE = 64
 LANES = 16
+SKEW = 2
 MESH = pl.DeviceIdType.MESH
 GRANT = 60 * 2**20
 
@@ -22,12 +23,30 @@
     return pieces, edges
 
 
-def kernel(counts, real_hbm, imag_hbm, coupling_hbm, strengths_hbm, offsets_hbm, real_out, imag_out,
-           own, near, far, coupling, strengths, offsets, turned, flat, weights, sigma, partial, rotated, dressed,
-           own_sem, small_sem, out_sem, far_send, far_recv, near_send, near_recv, halo_send, halo_recv, ack):
+def paired(real, imag):
+    return jnp.concatenate(
+        [jnp.concatenate([real, imag], axis=1), jnp.concatenate([-imag, real], axis=1)], axis=0)
+
+
+def product_of(green_real, green_imag, real, imag):
+    return jnp.dot(jnp.concatenate([green_real, green_imag], axis=1), paired(real, imag),
+                   preferred_element_type=jnp.float32).astype(jnp.bfloat16)
+
+
+def dressed_of(real, imag, prod):
+    back = jnp.dot(prod, paired(real, imag), preferred_element_type=jnp.float32)
+    orbitals = real.shape[-1]
+    return ((real.astype(jnp.float32) + back[:, :orbitals]).astype(jnp.bfloat16),
+            (imag.astype(jnp.float32) + back[:, orbitals:]).astype(jnp.bfloat16))
+
+
+def kernel(counts, real_hbm, imag_hbm, coupling_hbm, strengths_hbm, offsets_hbm, real_out, imag_out, sigma_out,
+           own, near, far, via, coupling, strengths, offsets, turned, flat, weights, sigma, partial, rotated, half, pending, final, dressed,
+           own_sem, small_sem, out_sem, final_sem, far_send, far_recv, near_send, near_recv, halo_send, halo_recv, via_recv, forward_send, ack):
     momenta, sections = counts
     hops, branches, orbitals = coupling.shape[0], coupling.shape[1], coupling.shape[-1]
     energies = own.shape[1]
+    last = energies - REACH - 1
     pieces, edges = pieces_of(energies)
     kz, en = lax.axis_index("kz"), lax.axis_index("en")
     odd = lax.rem(kz, 2)
@@ -65,6 +84,16 @@
         return pltpu.make_async_remote_copy(
             source, near.at[part, rows],
             near_send.at[part], near_recv.at[piece], device_id=(partner, en), device_id_type=MESH)
+
+    def via_copy(part):
+        return pltpu.make_async_remote_copy(
+            sources[part].at[0, pl.ds(last, 1)], via.at[part], near_send.at[part], via_recv,
+            device_id=(partner, en), device_id_type=MESH)
+
+    def forward_copy():
+        return pltpu.make_async_remote_copy(
+            via, near.at[:, pl.ds(REACH + last, 1)], forward_send, near_recv.at[len(pieces) - 1],
+            device_id=(ahead, en), device_id_type=MESH)
 
     def halo_copy(hop, side):
         field = fields[hop]
@@ -99,6 +128,12 @@
                     near_copy(piece, *pieces[piece], part, False).start()
 
     send_far(0, edges)
+
+    @pl.when(odd == 1)
+    def _():
+        for part in range(2):
+            via_copy(part).start()
+
     send_near(0, edges)
     send_far(edges, len(pieces))
     send_near(edges, len(pieces))
@@ -111,15 +146,22 @@
     def _():
         pl.semaphore_wait(ack.at[1], 1)
 
-    def arrive(piece, start, size):
+    def arrive_far(piece, start, size, relay=True):
         for part in range(2):
             far_copy(piece, start, size, part).wait_recv()
 
-            @pl.when(odd == 1)
-            def _(part=part):
-                near_copy(piece, start, size, part, True).start()
+            if relay:
+                @pl.when(odd == 1)
+                def _(part=part):
+                    near_copy(piece, start, size, part, True).start()
+
+    def arrive_near(piece, start, size):
         rows = pl.ds(REACH + start, size)
         pltpu.make_async_copy(near.at[:, rows], near.at[:, rows], near_recv.at[piece]).wait()
+
+    def arrive(piece, start, size):
+        arrive_far(piece, start, size)
+        arrive_near(piece, start, size)
 
     zeros = jnp.zeros((2, REACH, orbitals, orbitals), jnp.bfloat16)
     blank = jnp.zeros((orbitals, orbitals), jnp.bfloat16)
@@ -177,50 +219,48 @@
         return [jnp.concatenate([made[:orbitals, side:side + orbitals], made[orbitals:, side:side + orbitals]], axis=1)
                 for side in (0, orbitals)]
 
-    def left(parts):
-        total = jnp.dot(jnp.concatenate([flat[place] for place in range(hops * branches)], axis=1),
-                        jnp.concatenate(parts, axis=0), preferred_element_type=jnp.float32).astype(jnp.bfloat16)
+    def left(parts, hop=None):
+        places = range(hops * branches) if hop is None else range(hop * branches, (hop + 1) * branches)
+        return jnp.dot(jnp.concatenate([flat[place] for place in places], axis=1),
+                       jnp.concatenate(parts, axis=0), preferred_element_type=jnp.float32)
+
+    def rounded(total):
+        total = total.astype(jnp.bfloat16)
         return total[:, :orbitals], total[:, orbitals:]
 
-    def paired(real, imag):
-        return jnp.concatenate(
-            [jnp.concatenate([real, imag], axis=1), jnp.concatenate([-imag, real], axis=1)], axis=0)
-
     def product(energy, real, imag):
-        return jnp.dot(jnp.concatenate([own[0, energy], own[1, energy]], axis=1), paired(real, imag),
-                       preferred_element_type=jnp.float32).astype(jnp.bfloat16)
+        return product_of(own[0, energy], own[1, energy], real, imag)
 
     def dress(energy, prod):
-        real, imag = own[0, energy], own[1, energy]
-        back = jnp.dot(prod, paired(real, imag), preferred_element_type=jnp.float32)
-        dressed[0, energy] = (real.astype(jnp.float32) + back[:, :orbitals]).astype(jnp.bfloat16)
-        dressed[1, energy] = (imag.astype(jnp.float32) + back[:, orbitals:]).astype(jnp.bfloat16)
-
-    def stage(energy, slot, before):
+        dressed[0, energy], dressed[1, energy] = dressed_of(own[0, energy], own[1, energy], prod)
+
+    def part_of(energy, hop):
+        parts = []
+        for pair in range(branches // 2):
+            parts += right(energy, hop, pair, every)
+        return left(parts, hop)
+
+    def stage(energy, slot, before, following):
         if before is not None:
             prod = product(before, sigma[1 - slot, 0], sigma[1 - slot, 1])
-        parts = []
-        for hop in range(hops):
-            for pair in range(branches // 2):
-                parts += right(energy, hop, pair, every)
-            if hop == 0 and before is not None:
-                dress(before, prod)
-        sigma[slot, 0], sigma[slot, 1] = left(parts)
-
-    last = energies - REACH - 1
-    tail = [e for e in range(last - REACH, energies) if e != last]
-
-    def begin(energy, until):
+        sigma[slot, 0], sigma[slot, 1] = rounded(pending[slot] + part_of(energy, 0))
+        if before is not None:
+            dress(before, prod)
+        if following is not None:
+            pending[slot] = sum(part_of(following, hop) for hop in range(1, hops))
+
+    tail = range(last - REACH, energies)
+
+    def begin(energy, until, hop):
         taps = [tap for tap in every if not until < energy + tap - REACH <= last]
-        for hop in range(hops):
-            for pair in range(branches // 2):
-                for branch, value in zip((2 * pair, 2 * pair + 1), right(energy, hop, pair, taps)):
-                    for part in range(2):
-                        partial[tail.index(energy), place_of(hop, branch), part] = (
-                            value[:, part * orbitals:(part + 1) * orbitals])
+        for pair in range(branches // 2):
+            for branch, value in zip((2 * pair, 2 * pair + 1), right(energy, hop, pair, taps)):
+                for part in range(2):
+                    partial[tail.index(energy), place_of(hop, branch), part] = (
+                        value[:, part * orbitals:(part + 1) * orbitals])
 
     def ready(energy):
-        return last - REACH if energy > last else energy - 1
+        return last - REACH if energy >= last else energy - 1
 
     def rotate(source, hop):
         rows = jnp.concatenate([fields[hop][0, REACH + source], fields[hop][1, REACH + source]], axis=0)
@@ -264,6 +304,11 @@
     jobs = [(hop, branch) for hop in range(hops) for branch in range(branches)]
     for piece in range(edges):
         arrive(piece, *pieces[piece])
+        if piece == 1:
+            @pl.when(odd == 0)
+            def _():
+                pltpu.make_async_copy(via, via, via_recv).wait()
+                forward_copy().start()
         if piece == REACH - 1:
             for hop in range(hops):
                 halo_out(hop, 0, has_high)
@@ -282,12 +327,16 @@
     stages = 0
 
     def step(energy):
-        stage(energy, energy % 2, energy - 1 if energy > 0 else None)
+        stage(energy, energy % 2, energy - 1 if energy > 0 else None, energy + SKEW if energy + SKEW < tail[0] else None)
 
     halo_in(0, has_low)
     count = last - 1 - 2 * REACH
+    for energy in range(SKEW):
+        arrive_far(piece + energy, start + energy, 1)
+        pending[energy % 2] = sum(part_of(energy, hop) for hop in range(1, hops))
     for energy in range(2 - count % 2):
-        arrive(piece, *pieces[piece])
+        arrive_far(piece + SKEW, start + SKEW, 1)
+        arrive_near(piece, start, 1)
         step(energy)
         stages, start, piece = stages + 1, start + 1, piece + 1
     pairs = (count - stages) // 2
@@ -299,9 +348,10 @@
     def body(index, carry):
         first = base_start + 2 * index
         for offset in range(2):
-            arrive(base_piece + 2 * index + offset, first + offset, 1)
+            arrive_far(base_piece + 2 * index + offset + SKEW, first + offset + SKEW, 1)
+            arrive_near(base_piece + 2 * index + offset, first + offset, 1)
             energy = first - REACH + offset
-            stage(energy, (parity + offset) % 2, energy - 1)
+            stage(energy, (parity + offset) % 2, energy - 1, energy + SKEW)
         for part in range(2):
             out_copy(first - REACH - 1, 2, part).start()
         return carry
@@ -311,80 +361,110 @@
     halo_in(1, has_high)
     upper = list(range(last + 1, energies))
     for energy in upper[:2]:
-        begin(energy, last - REACH)
+        for hop in range(hops):
+            begin(energy, last - REACH, hop)
     lax.fori_loop(split, pairs, body, 0)
     for energy in upper[2:]:
-        begin(energy, last - REACH)
+        for hop in range(hops):
+            begin(energy, last - REACH, hop)
     piece, start, stages = piece + 2 * pairs, start + 2 * pairs, stages + 2 * pairs
 
+    def opened(source, hop):
+        if last - REACH <= source + 1 < last:
+            begin(source + 1, source, hop)
+        if source == last - REACH:
+            begin(last, source, hop)
+        if source > last - REACH:
+            rotate(source, hop)
+
+    def late(energy, hop):
+        return left([jnp.concatenate([updated(energy, hop, branch, part) for part in range(2)], axis=1)
+                     for branch in range(branches)], hop)
+
+    def halves():
+        for index, energy in enumerate(tail):
+            half[index] = sum(late(energy, hop) for hop in range(1, hops))
+
+    for source in range(start, start + SKEW):
+        for hop in range(1, hops):
+            opened(source, hop)
     for source in range(start, last):
-        arrive(piece, source, 1)
+        if source + SKEW <= last:
+            arrive_far(piece + SKEW, source + SKEW, 1, source + SKEW < last)
+        else:
+            halves()
+        arrive_near(piece, source, 1)
         step(stages)
-        opened = source + 1
-        if last - REACH <= opened < last:
-            begin(opened, source)
-        if source > last - REACH:
-            for hop in range(hops):
-                rotate(source, hop)
+        opened(source, 0)
+        if source + SKEW <= last:
+            for hop in range(1, hops):
+                opened(source + SKEW, hop)
         out(stages - 1, 1)
         stages += 1
         piece += 1
-    stage(last, stages % 2, stages - 1)
-    out(stages - 1, 1)
-
     for side, cond in ((0, has_high), (1, has_low)):
         @pl.when(cond)
         def _(side=side):
             for hop in range(hops):
                 halo_copy(hop, side).wait_send()
-    arrive(piece, last, 1)
-    for hop in range(hops):
-        rotate(last, hop)
-    waiting = [(last, product(last, sigma[stages % 2, 0], sigma[stages % 2, 1]))]
-    sums = []
-    for energy in tail + [None, None]:
-        made = None
-        if energy is not None:
-            parts = [jnp.concatenate([updated(energy, hop, branch, part) for part in range(2)], axis=1)
-                     for hop, branch in jobs]
-            made = (energy, *left(parts))
-        turn = waiting.pop(0) if waiting else None
-        if sums:
-            done = sums.pop(0)
-            waiting.append((done[0], product(*done)))
-        if made is not None:
-            sums.append(made)
-        if turn is not None:
-            dress(*turn)
-            out(turn[0], 1)
+    before = stages - 1
+    dress(before, product(before, sigma[before % 2, 0], sigma[before % 2, 1]))
+    out(before, 1)
+    arrive_near(piece, last, 1)
+    rotate(last, 0)
+
+    def final_copy(first, size):
+        rows = pl.ds(first, size)
+        return pltpu.make_async_copy(final.at[rows], sigma_out.at[rows], final_sem)
+
+    for index, energy in enumerate(tail):
+        final[index, 0], final[index, 1] = rounded(half[index] + late(energy, 0))
+        final_copy(index, 1).start()
 
     for part in range(2):
         far_copy(0, 0, energies, part).wait_send()
         near_copy(0, 0, energies, part, False).wait_send()
-        out_copy(0, energies, part).wait()
-
-
-def deliver(real_in, imag_in, real_out, imag_out, held, in_sem, out_sem):
-    chunks = held.shape[1]
-    size = held.shape[2]
-    refs = ((real_in, real_out), (imag_in, imag_out))
-
-    def fetch(part, chunk):
-        return pltpu.make_async_copy(
-            refs[part][0].at[0, pl.ds(chunk * size, size)], held.at[part, chunk], in_sem.at[part, chunk])
-
-    def store(part, chunk):
-        return pltpu.make_async_copy(
-            held.at[part, chunk], refs[part][1].at[0, pl.ds(chunk * size, size)], out_sem.at[part, chunk])
-
-    order = [(part, chunk) for chunk in range(chunks) for part in range(2)]
-    for key in order:
-        fetch(*key).start()
-    for key in order:
-        fetch(*key).wait()
-        store(*key).start()
-    for key in order:
-        store(*key).wait()
+        out_copy(0, stages, part).wait()
+    final_copy(0, len(tail)).wait()
+
+    @pl.when(odd == 0)
+    def _():
+        forward_copy().wait_send()
+
+
+def deliver(real_in, imag_in, sigma_in, real_hbm, imag_hbm, real_out, imag_out,
+            held, own, sigma, dressed, own_sem, sigma_sem, in_sem, out_sem):
+    count, early = sigma.shape[0], held.shape[1]
+    ins, greens, outs = (real_in, imag_in), (real_hbm, imag_hbm), (real_out, imag_out)
+    blocks = [(0, count // 3), (count // 3, count - count // 3)]
+
+    def own_copy(part, block):
+        return pltpu.make_async_copy(greens[part].at[0, pl.ds(early + blocks[block][0], blocks[block][1])],
+                                     own.at[part, pl.ds(*blocks[block])], own_sem.at[block, part])
+
+    def sigma_copy(block):
+        return pltpu.make_async_copy(sigma_in.at[pl.ds(*blocks[block])], sigma.at[pl.ds(*blocks[block])], sigma_sem.at[block])
+
+    fetches = [pltpu.make_async_copy(ins[part].at[0], held.at[part], in_sem.at[part]) for part in range(2)]
+    arrivals = [[sigma_copy(block), own_copy(0, block), own_copy(1, block)] for block in range(2)]
+    for copy in (*arrivals[0], *arrivals[1], *fetches):
+        copy.start()
+    for block, (first, size) in enumerate(blocks):
+        for copy in arrivals[block]:
+            copy.wait()
+        if block == 1:
+            for part in range(2):
+                fetches[part].wait()
+                pltpu.make_async_copy(held.at[part], outs[part].at[0, pl.ds(0, early)], out_sem.at[part]).start()
+        prods = [product_of(own[0, index], own[1, index], sigma[index, 0], sigma[index, 1])
+                 for index in range(first, first + size)]
+        for index, prod in enumerate(prods, first):
+            dressed[0, index], dressed[1, index] = dressed_of(own[0, index], own[1, index], prod)
+        for part in range(2):
+            pltpu.make_async_copy(dressed.at[part, pl.ds(first, size)],
+                                  outs[part].at[0, pl.ds(early + first, size)], out_sem.at[part]).start()
+    for part in range(2):
+        pltpu.make_async_copy(outs[part].at[0], outs[part].at[0], out_sem.at[part]).wait()
 
 
 def shards(counts, green_real, green_imag, coupling, strengths, offsets):
@@ -396,16 +476,20 @@
     chunks = len(pieces)
     square = (orbitals, orbitals)
     extended = (2, energies + 2 * REACH) + square
+    count = 2 * REACH + 1
+    early = energies - count
     shapes = [jax.ShapeDtypeStruct(green_real.shape, jnp.bfloat16)] * 2
-    dressed = pl.pallas_call(
+    made = pl.pallas_call(
         functools.partial(kernel, counts),
-        out_shape=shapes,
+        out_shape=[jax.ShapeDtypeStruct((1, early) + square, jnp.bfloat16)] * 2
+        + [jax.ShapeDtypeStruct((count, 2) + square, jnp.bfloat16)],
         in_specs=[anywhere] * 5,
-        out_specs=[anywhere] * 2,
+        out_specs=[anywhere] * 3,
         scratch_shapes=[
             pltpu.VMEM((2, energies) + square, jnp.bfloat16),
             pltpu.VMEM(extended, jnp.bfloat16),
             pltpu.VMEM(extended, jnp.bfloat16),
+            pltpu.VMEM((2, 1) + square, jnp.bfloat16),
             pltpu.VMEM(coupling.shape, jnp.bfloat16),
             pltpu.SMEM(strengths.shape, jnp.float32),
             pltpu.SMEM(offsets.shape, jnp.int32),
@@ -413,30 +497,35 @@
             pltpu.VMEM((hops * branches,) + square, jnp.bfloat16),
             pltpu.VMEM((hops * branches * TAPS, LANES, orbitals), jnp.bfloat16),
             pltpu.VMEM((2, 2) + square, jnp.bfloat16),
-            pltpu.VMEM((2 * REACH, hops * branches, 2) + square, jnp.bfloat16),
+            pltpu.VMEM((2 * REACH + 1, hops * branches, 2) + square, jnp.bfloat16),
             pltpu.VMEM((REACH, hops * branches, 2) + square, jnp.bfloat16),
-            pltpu.VMEM((2, energies) + square, jnp.bfloat16),
-            dma((2,)), dma((3,)), dma((2,)),
+            pltpu.VMEM((2 * REACH + 1, orbitals, 2 * orbitals), jnp.float32),
+            pltpu.VMEM((2, orbitals, 2 * orbitals), jnp.float32),
+            pltpu.VMEM((count, 2) + square, jnp.bfloat16),
+            pltpu.VMEM((2, early) + square, jnp.bfloat16),
+            dma((2,)), dma((3,)), dma((2,)), dma,
             dma((2,)), dma((chunks, 2)),
             dma((2,)), dma((chunks,)),
-            dma((hops, 2)), dma((hops, 2)),
+            dma((hops, 2)), dma((hops, 2)), dma, dma,
             pltpu.SemaphoreType.REGULAR((2,)),
         ],
         compiler_params=pltpu.CompilerParams(
             collective_id=0, has_side_effects=True, vmem_limit_bytes=GRANT),
     )(green_real, green_imag, coupling, strengths, offsets)
-    parts = 3 if energies % 3 == 0 else 1
     return pl.pallas_call(
         deliver,
         out_shape=shapes,
-        in_specs=[anywhere] * 2,
+        in_specs=[anywhere] * 5,
         out_specs=[anywhere] * 2,
         scratch_shapes=[
-            pltpu.VMEM((2, parts, energies // parts) + square, jnp.bfloat16),
-            dma((2, parts)), dma((2, parts)),
+            pltpu.VMEM((2, early) + square, jnp.bfloat16),
+            pltpu.VMEM((2, count) + square, jnp.bfloat16),
+            pltpu.VMEM((count, 2) + square, jnp.bfloat16),
+            pltpu.VMEM((2, count) + square, jnp.bfloat16),
+            dma((2, 2)), dma((2,)), dma((2,)), dma((2,)),
         ],
         compiler_params=pltpu.CompilerParams(vmem_limit_bytes=GRANT),
-    )(*dressed)
+    )(*made, green_real, green_imag)
 
 
 def solution(mesh):

time: 51.6 us -> 50.5 us (0.979)
  Pallas kernels: 50.8 us -> 49.6 us
    pallas_call x2, Pallas kernels: 50.8 us -> 49.6 us  [the longest x1 46.7 us: shards(): pl.pallas_call(functools.partial(kernel, counts), out_shape=[jax.ShapeDty...]
where the time goes in v3:
time: 50.5 us; the launch traced here: 50.4 us
  Pallas kernels  49.6 us (98%)
  between operations  0.8 us (2%)
    pallas_call x1, Pallas kernels, shards(): pl.pallas_call(functools.partial(kernel, counts), out_shape=[jax.ShapeDty...  46.7 us
    pallas_call x1, Pallas kernels, shards(): pl.pallas_call(deliver, out_shape=shapes, in_specs=[anywhere] * 5, out_sp...  2.88 us

profile of v3, /device:TPU:0, one launch (start us, length us, event | category | flops | bytes accessed | tf_op | source)
XLA Modules:
  0.0 50.4 jit_solution(14439046836287245346)
XLA Ops:
  0.6 46.7 %shard_map.68 = (bf16[1,15,128,128]{3,2,1,0:T(8,128)(2,1)}, bf16[1,15,128,128]{3,2,1,0:T(8,128)(2,1)}, bf16[9,2,128,128]{3,2,1,0:T(8,128)(2,1)}) custom-call(bf16[1,24,128,128]{3,2,1,0:T(8,128)(2,1)} %real_hbm.3, bf16[1,24,128,128]{3,2,1,0:T(8,128)(2,1)} %imag_hbm.3, bf16[2,4,1,128,128]{4,3,2,1,0:T(8,128)(2,1)} %coupling_hbm.1, f32[2,4,8]{2,1,0:T(4,128)} %strengths_hbm.1, ...), custom_call_target="tpu_custom_call" | custom-call | tf_op jit(solution)/shard_map/pallas_call | solution.py:482
  47.3 2.9 %shard_map.69 = (bf16[1,24,128,128]{3,2,1,0:T(8,128)(2,1)}, bf16[1,24,128,128]{3,2,1,0:T(8,128)(2,1)}) custom-call(bf16[1,15,128,128]{3,2,1,0:T(8,128)(2,1)} %get-tuple-element.5.real_in, bf16[1,15,128,128]{3,2,1,0:T(8,128)(2,1)} %get-tuple-element.6.imag_in, bf16[9,2,128,128]{3,2,1,0:T(8,128)(2,1)} %get-tuple-element.7.sigma_in, ...), custom_call_target="tpu_custom_call" | custom-call | tf_op jit(solution)/shard_map/pallas_call | solution.py:515

commit v4 on v3

--- a/solution.py
+++ b/solution.py
@@ -69,8 +69,6 @@
 
     smalls = [pltpu.make_async_copy(a, b, small_sem.at[i]) for i, (a, b) in enumerate(
         ((coupling_hbm, coupling), (strengths_hbm, strengths), (offsets_hbm, offsets)))]
-    for copy in smalls:
-        copy.start()
     pl.semaphore_wait(barrier, 1 + odd + has_low.astype(jnp.int32))
 
     def far_copy(piece, start, size, part):
@@ -135,6 +133,8 @@
             via_copy(part).start()
 
     send_near(0, edges)
+    for copy in smalls:
+        copy.start()
     send_far(edges, len(pieces))
     send_near(edges, len(pieces))
 
@@ -391,8 +391,10 @@
     for source in range(start, last):
         if source + SKEW <= last:
             arrive_far(piece + SKEW, source + SKEW, 1, source + SKEW < last)
-        else:
+        elif source == last - 1:
             halves()
+            arrive_near(piece + 1, last, 1)
+            rotate(last, 0)
         arrive_near(piece, source, 1)
         step(stages)
         opened(source, 0)
@@ -410,8 +412,6 @@
     before = stages - 1
     dress(before, product(before, sigma[before % 2, 0], sigma[before % 2, 1]))
     out(before, 1)
-    arrive_near(piece, last, 1)
-    rotate(last, 0)
 
     def final_copy(first, size):
         rows = pl.ds(first, size)

time: 50.5 us -> 50.4 us (level)
  no operation moved by 1% of the time
where the time goes in v4:
time: 50.4 us; the launch traced here: 50.2 us
  Pallas kernels  49.4 us (98%)
  between operations  0.8 us (2%)
    pallas_call x1, Pallas kernels, shards(): pl.pallas_call(functools.partial(kernel, counts), out_shape=[jax.ShapeDty...  46.6 us
    pallas_call x1, Pallas kernels, shards(): pl.pallas_call(deliver, out_shape=shapes, in_specs=[anywhere] * 5, out_sp...  2.88 us

profile of v4, /device:TPU:0, one launch (start us, length us, event | category | flops | bytes accessed | tf_op | source)
XLA Modules:
  0.0 50.2 jit_solution(362951687871214448)
XLA Ops:
  0.6 46.6 %shard_map.68 = (bf16[1,15,128,128]{3,2,1,0:T(8,128)(2,1)}, bf16[1,15,128,128]{3,2,1,0:T(8,128)(2,1)}, bf16[9,2,128,128]{3,2,1,0:T(8,128)(2,1)}) custom-call(bf16[1,24,128,128]{3,2,1,0:T(8,128)(2,1)} %real_hbm.3, bf16[1,24,128,128]{3,2,1,0:T(8,128)(2,1)} %imag_hbm.3, bf16[2,4,1,128,128]{4,3,2,1,0:T(8,128)(2,1)} %coupling_hbm.1, f32[2,4,8]{2,1,0:T(4,128)} %strengths_hbm.1, ...), custom_call_target="tpu_custom_call" | custom-call | tf_op jit(solution)/shard_map/pallas_call | solution.py:482
  47.2 2.9 %shard_map.69 = (bf16[1,24,128,128]{3,2,1,0:T(8,128)(2,1)}, bf16[1,24,128,128]{3,2,1,0:T(8,128)(2,1)}) custom-call(bf16[1,15,128,128]{3,2,1,0:T(8,128)(2,1)} %get-tuple-element.5.real_in, bf16[1,15,128,128]{3,2,1,0:T(8,128)(2,1)} %get-tuple-element.6.imag_in, bf16[9,2,128,128]{3,2,1,0:T(8,128)(2,1)} %get-tuple-element.7.sigma_in, ...), custom_call_target="tpu_custom_call" | custom-call | tf_op jit(solution)/shard_map/pallas_call | solution.py:515
